TPU v7x, 32 devices: a whole 2x2x4 slice. The times are simulated.
32 devices in a mesh: grp: 4 (over y, x), slab: 8 (over z, core).
Axes of the slice: x: 2, y: 2, z: 4, core: 2. Of those that a mesh axis runs over, the one named last changes fastest.
Arguments:
- fields: float32 [64, 64, 8, 128], P('grp', 'slab'), may hold values from -6 to 6
- velocity: int32 [3, 64, 8, 128], P(None, 'slab'), may hold values from -2 to 2
- diffusivity: float32 [64, 8, 128], P('slab'), may hold values from 0.005 to 0.04
- sensor_offsets: int32 [49152], P('slab'), may hold values from 0 to 8191
- sensor_counts: int32 [8], P('slab'), may hold values from 1 to 6144, 16384 in all
- observations: float32 [49152], P('slab'), may hold values from -6 to 6
- noise_scale: float32 [49152], P('slab'), may hold values from 2 to 20
- perturbation: float32 [64, 49152], P('grp', 'slab'), may hold values from -6 to 6
Outputs:
- updated: float32 [64, 64, 8, 128], P('grp', 'slab')
Inputs may be any that keep to these rules, and one draw needn't show every extreme that they name: `sensor_counts`: the counts sum to 16384 and the largest is exactly 6144. `sensor_offsets`: slots at or past their slab's count are unused.
All inputs are finite; a program needn't handle non-finite values. No bound on the sum of `sensor_counts` on one device may be relied on, other than what follows from the above.
Results may differ from a plain program's by a relative error of at most 0.00011.
Values sent between devices are 32-bit elements; how exact they have to be, the bound alone decides.
A program may use at most 64 MiB of HBM per device.

v0:
```python
import math
import jax
import jax.numpy as jnp
from jax import lax
from jax.sharding import PartitionSpec as P

STEPS = 2
COURANT = 0.12


def extended_2(array, sides, width):
    for axis, dim in sides:
        size, length = (lax.axis_size(axis), array.shape[dim])
        up = [(i, (i + 1) % size) for i in range(size - 1)]
        down = [(j, i) for i, j in up]
        last = lax.slice_in_dim(array, length - width, length, axis=dim)
        initial = lax.slice_in_dim(array, 0, width, axis=dim)
        before = lax.ppermute(last, axis, up)
        after = lax.ppermute(initial, axis, down)
        array = jnp.concatenate([before, array, after], axis=dim)
    return array


def upwind(courant, center, lower_side, upper_side):
    return jnp.maximum(courant, 0.0) * (center - lower_side) + jnp.minimum(courant, 0.0) * (
        upper_side - center
    )


def advance(extended, courant, diffusivity):
    center = extended[:, 1:-1]
    below = extended[:, :-2]
    above = extended[:, 2:]
    south = jnp.roll(center, 1, axis=2)
    north = jnp.roll(center, -1, axis=2)
    west = jnp.roll(center, 1, axis=3)
    east = jnp.roll(center, -1, axis=3)
    transport = upwind(courant[0], center, below, above) + upwind(courant[1], center, south, north)
    transport = transport + upwind(courant[2], center, west, east)
    laplace = below + above + south + north + west + east - 6.0 * center
    return center - transport + diffusivity * laplace


def solve_weights(gram_matrix, cross_matrix, spread_root):
    order = gram_matrix.shape[0]
    index_row = jnp.arange(order, dtype=jnp.int32)
    system = jnp.eye(order, dtype=jnp.float32) + gram_matrix

    def factor_column(column, lower_factor):
        row_here = lax.dynamic_slice_in_dim(lower_factor, column, 1, 0)[0]
        needed = lax.dynamic_slice_in_dim(system, column, 1, 1)[:, 0]
        needed = needed - jnp.dot(
            lower_factor,
            row_here,
            precision=lax.Precision.HIGHEST,
            preferred_element_type=jnp.float32,
        )
        pivot = jnp.sqrt(lax.dynamic_slice_in_dim(needed, column, 1, 0)[0])
        values = jnp.where(index_row >= column, needed / pivot, 0.0)
        marker = (index_row == column).astype(jnp.float32)
        return lower_factor + values[:, None] * marker[None, :]

    lower_factor = lax.fori_loop(0, order, factor_column, jnp.zeros((order, order), jnp.float32))

    def forward_row(row, solved):
        factor_row = lax.dynamic_slice_in_dim(lower_factor, row, 1, 0)[0]
        pivot = lax.dynamic_slice_in_dim(factor_row, row, 1, 0)[0]
        given = lax.dynamic_slice_in_dim(cross_matrix, row, 1, 0)[0]
        value = (
            given
            - jnp.dot(
                factor_row,
                solved,
                precision=lax.Precision.HIGHEST,
                preferred_element_type=jnp.float32,
            )
        ) / pivot
        return lax.dynamic_update_slice_in_dim(solved, value[None, :], row, 0)

    middle = lax.fori_loop(0, order, forward_row, jnp.zeros_like(cross_matrix))

    def backward_row(turn, solved):
        row = order - 1 - turn
        factor_col = lax.dynamic_slice_in_dim(lower_factor, row, 1, 1)[:, 0]
        pivot = lax.dynamic_slice_in_dim(factor_col, row, 1, 0)[0]
        given = lax.dynamic_slice_in_dim(middle, row, 1, 0)[0]
        value = (
            given
            - jnp.dot(
                factor_col,
                solved,
                precision=lax.Precision.HIGHEST,
                preferred_element_type=jnp.float32,
            )
        ) / pivot
        return lax.dynamic_update_slice_in_dim(solved, value[None, :], row, 0)

    result = lax.fori_loop(0, order, backward_row, jnp.zeros_like(cross_matrix))
    return result / spread_root


def ensemble_parts(centered, misfit_rows):
    gram_part = jnp.dot(
        centered, centered.T, precision=lax.Precision.HIGHEST, preferred_element_type=jnp.float32
    )
    cross_part = jnp.dot(
        centered, misfit_rows.T, precision=lax.Precision.HIGHEST, preferred_element_type=jnp.float32
    )
    return (gram_part, cross_part)


def sample_cells(current, sensor_offsets):
    members_here = current.shape[0]
    row_count = current.shape[1] * current.shape[2]
    width = current.shape[3]
    planes = current.reshape(members_here, row_count, width)
    slot_total = sensor_offsets.shape[0]
    block_size = math.gcd(slot_total, 512)
    block_count = slot_total // block_size
    row_ids = jnp.arange(row_count, dtype=jnp.int32)
    col_ids = jnp.arange(width, dtype=jnp.int32)

    def pick_block(offsets):
        row_pick = offsets // width
        col_pick = offsets % width
        col_table = (col_ids[:, None] == col_pick[None, :]).astype(jnp.float32)
        chosen = jnp.einsum(
            "qng,gl->qnl",
            planes,
            col_table,
            precision=lax.Precision.HIGHEST,
            preferred_element_type=jnp.float32,
        )
        row_table = (row_ids[:, None] == row_pick[None, :]).astype(jnp.float32)
        return jnp.sum(chosen * row_table[None, :, :], axis=1)

    blocks = lax.map(pick_block, sensor_offsets.reshape(block_count, block_size))
    return jnp.transpose(blocks, (1, 0, 2)).reshape(members_here, slot_total)


def local(
    fields,
    velocity,
    diffusivity,
    sensor_offsets,
    sensor_counts,
    observations,
    noise_scale,
    perturbation,
):
    members_here = fields.shape[0]
    group_count = lax.axis_size("grp")
    members_all = members_here * group_count
    spread_root = math.sqrt(members_all - 1)
    courant = velocity.astype(jnp.float32) * COURANT
    current = fields
    for counter in range(STEPS):
        extended = extended_2(current, (("slab", 1),), 1)
        current = advance(extended, courant, diffusivity)
    cell_total = current.shape[1] * current.shape[2] * current.shape[3]
    flattened = current.reshape(members_here, cell_total)
    slot_total = sensor_offsets.shape[0]
    live_mask = (jnp.arange(slot_total, dtype=jnp.int32) < sensor_counts[0]).astype(jnp.float32)
    predicted = sample_cells(current, sensor_offsets)
    scaled = live_mask * predicted / noise_scale
    misfit = live_mask * ((observations - predicted) / noise_scale + perturbation)
    scaled_sum = lax.psum(jnp.sum(scaled, axis=0), "grp")
    leading = (scaled - scaled_sum / members_all) / spread_root
    gathered_lead, gathered_misfit = (
        lax.all_gather(leading, "grp", axis=0, tiled=True),
        lax.all_gather(misfit, "grp", axis=0, tiled=True),
    )
    gram_part, cross_part = ensemble_parts(gathered_lead, gathered_misfit)
    gram_matrix, cross_matrix = lax.psum((gram_part, cross_part), "slab")
    weights = solve_weights(gram_matrix, cross_matrix, spread_root)
    group_index = lax.axis_index("grp")
    own_weights = lax.dynamic_slice_in_dim(weights, group_index * members_here, members_here, 1)
    increment = jnp.dot(
        own_weights.T,
        lax.all_gather(flattened, "grp", axis=0, tiled=True),
        precision=lax.Precision.HIGHEST,
        preferred_element_type=jnp.float32,
    )
    return (flattened + increment).reshape(current.shape)


def solution(mesh):
    return jax.shard_map(
        local,
        mesh=mesh,
        in_specs=(
            P("grp", "slab", None, None),
            P(None, "slab", None, None),
            P("slab", None, None),
            P("slab"),
            P("slab"),
            P("slab"),
            P("slab"),
            P("grp", "slab"),
        ),
        out_specs=P("grp", "slab", None, None),
        check_vma=False,
    )
```

profile of v0, /device:TPU:0, one launch (start us, length us, event | category | flops | bytes accessed | tf_op | source)
XLA Modules:
  0.0 487.9 jit_solution(3557998516879532501)
XLA Ops:
  6.5 1.6 fusion.75
  8.1 3.0 collective-permute-start
  11.1 1.3 collective-permute-start.1
  12.4 1.3 fusion.72
  13.9 1.0 fusion.74
  15.7 0.9 convert_multiply_fusion
  17.3 1.3 reshape.81
  19.9 1.4 div.111
  21.9 2.0 fusion.51
  24.5 4.6 collective-permute-start.2
  29.1 1.3 collective-permute-start.3
  30.5 3.0 collective-permute-done.3
  34.4 31.0 %while.62 = (s32[]{:T(128)}, f32[12,16,512]{2,1,0:T(8,128)S(1)}, s32[12,512]{1,0:T(8,128)}, f32[16,64,128]{2,1,0:T(8,128)S(1)}, s32[]{:T(128)}) while((s32[]{:T(128)}, f32[12,16,512]{2,1,0:T(8,128)S(1)}, s32[12,512]{1,0:T(8,128)}, f32[16,64,128]{2,1,0:T(8,128)S(1)}, s32[]{:T(128)}) %tuple.168), condition=%wide.region_2.3_spmd.clone, body=%wide.region_0.2_spmd.clone.sunk | while | flops 806489600 | bytes 901193 | solution.py:137
  35.9 1.0 fusion.109
  38.5 1.0 fusion.109
  41.1 1.0 fusion.109
  43.7 1.0 fusion.109
  46.3 1.0 fusion.109
  48.9 1.1 fusion.109
  51.5 1.0 fusion.109
  54.0 1.0 fusion.109
  56.6 1.0 fusion.109
  59.2 1.1 fusion.109
  61.8 1.0 fusion.109
  64.4 1.0 fusion.109
  65.7 16.3 %psum.21 = f32[6144]{0:T(1024)S(1)} all-reduce(f32[6144]{0:T(1024)S(1)} %reduce_sum.24), channel_id=1, replica_groups=mesh['grp'=4,'slab'=8] {'grp'}, use_global_device_ids=true, to_apply=%region_4.5 | all-reduce | flops 6144 | bytes 49152 | tf_op jit(solution)/shard_map/psum | solution.py:167
  82.0 1.0 add_multiply_fusion
  83.8 1.1 copy.20
  85.0 29.7 %all-gather.4.cloned.1.call-done = f32[64,6144]{1,0:T(8,128)} async-done(((f32[16,6144]{1,0:T(8,128)}), f32[64,6144]{1,0:T(8,128)}) %all-gather.4.cloned.1.call-update) | async-done | bytes 1572880 | tf_op jit(solution)/shard_map/all_gather | solution.py:170
  114.6 3.4 fusion.77
  118.0 29.3 %all-gather.6.cloned.1.call-done = f32[64,6144]{1,0:T(8,128)} async-done(((f32[16,6144]{1,0:T(8,128)}), f32[64,6144]{1,0:T(8,128)}) %all-gather.6.cloned.1.call-update) | async-done | bytes 1572880 | tf_op jit(solution)/shard_map/all_gather | solution.py:171
  147.3 2.8 fusion.76
  150.1 28.9 %all-reduce = (f32[64,64]{1,0:T(8,128)S(1)}, f32[64,64]{1,0:T(8,128)S(1)}) all-reduce(f32[64,64]{1,0:T(8,128)S(1)} %fusion.76, f32[64,64]{1,0:T(8,128)S(1)} %fusion.77), channel_id=1, replica_groups=mesh['grp'=4,'slab'=8] {'slab'}, use_global_device_ids=true, to_apply=%region_8.9 | all-reduce | flops 8192 | bytes 65536 | tf_op jit(solution)/shard_map/psum | solution.py:174
  179.1 105.9 %while.63 = (s32[]{:T(128)}, f32[64,64]{1,0:T(8,128)S(1)}, f32[64,64]{0,1:T(8,128)S(1)}, s32[]{:T(128)}, s32[]{:T(128)}) while((s32[]{:T(128)}, f32[64,64]{1,0:T(8,128)S(1)}, f32[64,64]{0,1:T(8,128)S(1)}, s32[]{:T(128)}, s32[]{:T(128)}) %tuple.153), condition=%wide.region_7.8_spmd.clone.clone, body=%wide.region_6.7_spmd.clone.clone.sunk | while | flops 65923 | bytes 101992 | solution.py:63
  285.1 96.0 %while.60 = (s32[]{:T(128)}, f32[64,64]{1,0:T(8,128)S(1)}, f32[64,64]{1,0:T(8,128)S(1)}, f32[64,64]{1,0:T(8,128)S(1)}, s32[]{:T(128)}, /*index=5*/s32[]{:T(128)}, s32[]{:T(128)}) while((s32[]{:T(128)}, f32[64,64]{1,0:T(8,128)S(1)}, f32[64,64]{1,0:T(8,128)S(1)}, f32[64,64]{1,0:T(8,128)S(1)}, s32[]{:T(128)}, /*index=5*/s32[]{:T(128)}, ...), condition=%wide.region_10.11_spmd, body=%wide.region_9.10_spmd.sunk | while | flops 49283 | bytes 36205 | solution.py:80
  285.8 0.8 fusion.102
  287.3 0.8 fusion.102
  288.8 0.8 fusion.102
  290.3 0.8 fusion.102
  291.8 0.8 fusion.102
  293.3 0.8 fusion.102
  294.8 0.8 fusion.102
  297.8 0.8 fusion.102
  299.3 0.8 fusion.102
  302.3 0.8 fusion.102
  303.8 0.8 fusion.102
  306.8 0.8 fusion.102
  308.3 0.8 fusion.102
  309.8 0.8 fusion.102
  311.3 0.8 fusion.102
  312.8 0.8 fusion.102
  314.3 0.8 fusion.102
  315.8 0.8 fusion.102
  317.3 0.8 fusion.102
  318.8 0.8 fusion.102
  320.3 0.8 fusion.102
  321.8 0.8 fusion.102
  323.3 0.8 fusion.102
  326.3 0.8 fusion.102
  327.8 0.8 fusion.102
  330.8 0.8 fusion.102
  381.1 96.4 %while.61 = (s32[]{:T(128)}, f32[64,64]{1,0:T(8,128)S(1)}, f32[64,64]{1,0:T(8,128)S(1)}, f32[64,64]{0,1:T(8,128)S(1)}, s32[]{:T(128)}, /*index=5*/s32[]{:T(128)}, s32[]{:T(128)}, s32[]{:T(128)}) while((s32[]{:T(128)}, f32[64,64]{1,0:T(8,128)S(1)}, f32[64,64]{1,0:T(8,128)S(1)}, f32[64,64]{0,1:T(8,128)S(1)}, s32[]{:T(128)}, ...), condition=%wide.region_12.13_spmd, body=%wide.region_11.12_spmd.sunk | while | flops 49287 | bytes 35751 | solution.py:98
  477.6 2.9 fusion.26
  480.5 0.9 copy.16
  (852 shorter events, 250.8 us)
Async XLA Ops:
  6.5 7.2 %copy-start = (f32[16,8,8,128]{3,2,1,0:T(8,128)S(1)}, f32[16,8,8,128]{3,2,1,0:T(8,128)}, u32[]{:S(2)}) copy-start(f32[16,8,8,128]{3,2,1,0:T(8,128)} %param.16) | copy-start | bytes 1572868
  6.5 108.1 %all-gather.4.cloned.1.call-start = ((), (), s32[]{:S(2)}) async-start(), calls=%async_computation | async-start | bytes 1966080 | tf_op jit(solution)/shard_map/all_gather | solution.py:170
  8.1 13.8 %collective-permute-start = (f32[16,1,8,128]{3,2,1,0:T(8,128)}, f32[16,1,8,128]{3,2,1,0:T(8,128)}, u32[]{:S(2)}, u32[]{:S(2)}) collective-permute-start(f32[16,1,8,128]{3,2,1,0:T(8,128)} %get-tuple-element.525), channel_id=1, source_target_pairs={{0,1},{1,2},{2,3},{3,4},{4,5},{5,6},{6,7},{8,9},{9,10},{10,11},{11... | collective-permute-start | bytes 196616 | tf_op jit(solution)/shard_map/ppermute | solution.py:18
  11.1 10.7 %collective-permute-start.1 = (f32[16,1,8,128]{3,2,1,0:T(8,128)}, f32[16,1,8,128]{3,2,1,0:T(8,128)}, u32[]{:S(2)}, u32[]{:S(2)}) collective-permute-start(f32[16,1,8,128]{3,2,1,0:T(8,128)} %get-tuple-element.526), channel_id=1, source_target_pairs={{1,0},{2,1},{3,2},{4,3},{5,4},{6,5},{7,6},{9,8},{10,9},{11,10},{12... | collective-permute-start | bytes 196616 | tf_op jit(solution)/shard_map/ppermute | solution.py:19
  24.2 9.3 %copy-start.3 = (f32[8,8,128]{2,1,0:T(8,128)S(1)}, f32[8,8,128]{2,1,0:T(8,128)}, u32[]{:S(2)}) copy-start(f32[8,8,128]{2,1,0:T(8,128)} %get-tuple-element.529) | copy-start | bytes 98308
  24.2 9.3 %copy-start.4 = (f32[8,8,128]{2,1,0:T(8,128)S(1)}, f32[8,8,128]{2,1,0:T(8,128)}, u32[]{:S(2)}) copy-start(f32[8,8,128]{2,1,0:T(8,128)} %get-tuple-element.530) | copy-start | bytes 98308
  24.2 9.3 %copy-start.5 = (f32[8,8,128]{2,1,0:T(8,128)S(1)}, f32[8,8,128]{2,1,0:T(8,128)}, u32[]{:S(2)}) copy-start(f32[8,8,128]{2,1,0:T(8,128)} %get-tuple-element.531) | copy-start | bytes 98308
  24.2 9.3 %copy-start.6 = (f32[8,8,128]{2,1,0:T(8,128)S(1)}, f32[8,8,128]{2,1,0:T(8,128)}, u32[]{:S(2)}) copy-start(f32[8,8,128]{2,1,0:T(8,128)} %get-tuple-element.532) | copy-start | bytes 98308
  24.3 9.3 %copy-start.7 = (f32[8,8,128]{2,1,0:T(8,128)S(1)}, f32[8,8,128]{2,1,0:T(8,128)}, u32[]{:S(2)}) copy-start(f32[8,8,128]{2,1,0:T(8,128)} %get-tuple-element.533) | copy-start | bytes 98308
  24.3 9.3 %copy-start.8 = (f32[8,8,128]{2,1,0:T(8,128)S(1)}, f32[8,8,128]{2,1,0:T(8,128)}, u32[]{:S(2)}) copy-start(f32[8,8,128]{2,1,0:T(8,128)} %get-tuple-element.534) | copy-start | bytes 98308
  24.3 9.3 %copy-start.9 = (f32[8,8,128]{2,1,0:T(8,128)S(1)}, f32[8,8,128]{2,1,0:T(8,128)}, u32[]{:S(2)}) copy-start(f32[8,8,128]{2,1,0:T(8,128)} %param.18) | copy-start | bytes 98308
  24.5 6.0 %collective-permute-start.2 = (f32[16,1,8,128]{3,2,1,0:T(8,128)S(1)}, f32[16,1,8,128]{3,2,1,0:T(8,128)S(1)}, u32[]{:S(2)}, u32[]{:S(2)}) collective-permute-start(f32[16,1,8,128]{3,2,1,0:T(8,128)S(1)} %get-tuple-element.515), channel_id=1, source_target_pairs={{0,1},{1,2},{2,3},{3,4},{4,5},{5,6},{6,7},{8,9},{9,10},{10,11},{11... | collective-permute-start | bytes 196616 | tf_op jit(solution)/shard_map/ppermute | solution.py:18
  29.1 4.4 collective-permute-start.3
  34.4 31.1 %copy-start.10 = (f32[12,512]{1,0:T(8,128)S(1)}, f32[12,512]{1,0:T(8,128)}, u32[]{:S(2)}) copy-start(f32[12,512]{1,0:T(8,128)} %fusion.61) | copy-start | bytes 73732
  34.4 31.1 %copy-start.11 = (f32[12,512]{1,0:T(8,128)S(1)}, f32[12,512]{1,0:T(8,128)}, u32[]{:S(2)}) copy-start(f32[12,512]{1,0:T(8,128)} %div.111) | copy-start | bytes 73732
  34.4 47.5 %copy-start.12 = (f32[6144]{0:T(1024)S(1)}, f32[6144]{0:T(1024)}, u32[]{:S(2)}) copy-start(f32[6144]{0:T(1024)} %param.22) | copy-start | bytes 73732
  34.4 47.5 %copy-start.13 = (f32[6144]{0:T(1024)S(1)}, f32[6144]{0:T(1024)}, u32[]{:S(2)}) copy-start(f32[6144]{0:T(1024)} %fusion.62) | copy-start | bytes 73732
  34.4 47.5 %copy-start.14 = (f32[6144]{0:T(1024)S(1)}, f32[6144]{0:T(1024)}, u32[]{:S(2)}) copy-start(f32[6144]{0:T(1024)} %param.21) | copy-start | bytes 73732
  65.5 16.5 %copy-start.2 = (f32[16,6144]{1,0:T(8,128)S(1)}, f32[16,6144]{1,0:T(8,128)}, u32[]{:S(2)}) copy-start(f32[16,6144]{1,0:T(8,128)} %param.23) | copy-start | bytes 1179652
  83.0 64.3 %all-gather.6.cloned.1.call-start = ((), (), s32[]{:S(2)}) async-start(), calls=%async_computation.1 | async-start | bytes 1966080 | tf_op jit(solution)/shard_map/all_gather | solution.py:171
  83.8 393.8 %all-gather.8.cloned.1.call-start = ((), (), s32[]{:S(2)}) async-start(), calls=%async_computation.2 | async-start | bytes 2621440 | tf_op jit(solution)/shard_map/all_gather | solution.py:180
  114.6 32.7 %copy-start.1 = (f32[64,6144]{1,0:T(8,128)S(1)}, f32[64,6144]{1,0:T(8,128)}, u32[]{:S(2)}) copy-start(f32[64,6144]{1,0:T(8,128)} %all-gather.4.cloned.1.call-done) | copy-start | bytes 4718596
Sparse Core Ops, SparseCore 0:
  83.1 31.4 all-gather.3
  116.5 30.8 all-gather.5
  149.2 35.2 all-gather.7
where the time goes:
time: 492 us; the launch traced here: 488 us
  local copies, waits for them, and re-layouts  140 us (28%)
  matrix products  134 us (27%)
  waiting for transfers between devices  62.7 us (13%)
  loops' own time  50.6 us (10%)
  blocking collectives  45.2 us (9%)
  other arithmetic  30.7 us (6%)
  between operations  14.2 us (3%)
  starting transfers between devices  10.3 us (2%)
    dot_general x64, matrix products, forward_row(): jnp.dot(factor_row, solved, precision=lax.Precision.HIGHEST, preferred_el...  51.5 us
    dot_general x64, matrix products, backward_row(): jnp.dot(factor_col, solved, precision=lax.Precision.HIGHEST, preferred_el...  51.5 us
    another operation x1, loops' own time, solve_weights(): lax.fori_loop(0, order, factor_column, jnp.zeros((order, order), jnp.floa...  47.1 us
    dynamic_slice x64, local copies, waits for them, and re-layouts, factor_column(): pivot = jnp.sqrt(lax.dynamic_slice_in_dim(needed, column, 1, 0)[0])  43.5 us
    dynamic_slice x64, local copies, waits for them, and re-layouts, forward_row(): pivot = lax.dynamic_slice_in_dim(factor_row, row, 1, 0)[0]  41.6 us
    dynamic_slice x64, local copies, waits for them, and re-layouts, backward_row(): pivot = lax.dynamic_slice_in_dim(factor_col, row, 1, 0)[0]  41.6 us
    all_gather x1, waiting for transfers between devices, local(): lax.all_gather(leading, 'grp', axis=0, tiled=True)  29.7 us
    all_gather x1, waiting for transfers between devices, local(): lax.all_gather(misfit, 'grp', axis=0, tiled=True)  29.3 us
  transfers between devices with their start and end apart: 7, of which 3 were waited for; matrix products, arithmetic and copies ran while one was open for 54% of the time, Pallas kernels for 0%

commit v1 on v0

--- a/solution.py
+++ b/solution.py
@@ -6,6 +6,19 @@
 
 STEPS = 2
 COURANT = 0.12
+
+
+def gather_around(x, axis, dim):
+    ways = lax.axis_size(axis)
+    up = [(d, (d + 1) % ways) for d in range(ways)]
+    down = [(d, (d - 1) % ways) for d in range(ways)]
+    earlier, later = ([x], [x])
+    for _ in range(ways // 2):
+        earlier.append(lax.ppermute(earlier[-1], axis, up))
+    for _ in range((ways - 1) // 2):
+        later.append(lax.ppermute(later[-1], axis, down))
+    line = jnp.concatenate([*earlier[::-1], *later[1:]], axis=dim)
+    return jnp.roll(line, (lax.axis_index(axis) - ways // 2) * x.shape[dim], axis=dim)
 
 
 def extended_2(array, sides, width):
@@ -167,7 +180,7 @@
     scaled_sum = lax.psum(jnp.sum(scaled, axis=0), "grp")
     leading = (scaled - scaled_sum / members_all) / spread_root
     gathered_lead, gathered_misfit = (
-        lax.all_gather(leading, "grp", axis=0, tiled=True),
+        gather_around(leading, "grp", 0),
         lax.all_gather(misfit, "grp", axis=0, tiled=True),
     )
     gram_part, cross_part = ensemble_parts(gathered_lead, gathered_misfit)

time: 492 us -> 436 us (0.89)
  waiting for transfers between devices: 62.7 us -> 37.9 us
  matrix products: 134 us -> 119 us
  local copies, waits for them, and re-layouts: 140 us -> 130 us
  loops' own time: 50.6 us -> 43.9 us
    ppermute x0 -> x3, waiting for transfers between devices: none -> 34.8 us  [the longest x2 21.2 us: gather_around(): earlier.append(lax.ppermute(earlier[-1], axis, up))]
    all_gather x1 -> x0, waiting for transfers between devices: 29.7 us -> none  [local(): lax.all_gather(leading, 'grp', axis=0, tiled=True)]
    all_gather x1, waiting for transfers between devices: 29.3 us -> 0.02 us  [local(): lax.all_gather(misfit, 'grp', axis=0, tiled=True)]
    another operation x1, loops' own time: 47.1 us -> 40.5 us  [solve_weights(): lax.fori_loop(0, order, factor_column, jnp.zeros((order, order), jnp.floa...]
    dot_general x64, matrix products: 51.5 us -> 44.9 us  [forward_row(): jnp.dot(factor_row, solved, precision=lax.Precision.HIGHEST, preferred_el...]
    dot_general x64, matrix products: 51.5 us -> 44.9 us  [backward_row(): jnp.dot(factor_col, solved, precision=lax.Precision.HIGHEST, preferred_el...]
  transfers between devices with their start and end apart: 7 -> 9, of which waited for: 3 -> 4; matrix products, arithmetic and copies ran while one was open for 54% -> 55% of each run, Pallas kernels for 0% -> 0%
where the time goes in v1:
time: 436 us; the launch traced here: 432 us
  local copies, waits for them, and re-layouts  130 us (30%)
  matrix products  119 us (27%)
  loops' own time  43.9 us (10%)
  blocking collectives  42.6 us (10%)
  waiting for transfers between devices  37.9 us (9%)
  other arithmetic  30.6 us (7%)
  between operations  14.5 us (3%)
  starting transfers between devices  13.2 us (3%)
    dot_general x64, matrix products, forward_row(): jnp.dot(factor_row, solved, precision=lax.Precision.HIGHEST, preferred_el...  44.9 us
    dot_general x64, matrix products, backward_row(): jnp.dot(factor_col, solved, precision=lax.Precision.HIGHEST, preferred_el...  44.9 us
    another operation x1, loops' own time, solve_weights(): lax.fori_loop(0, order, factor_column, jnp.zeros((order, order), jnp.floa...  40.5 us
    dynamic_slice x64, local copies, waits for them, and re-layouts, factor_column(): pivot = jnp.sqrt(lax.dynamic_slice_in_dim(needed, column, 1, 0)[0])  39.1 us
    dynamic_slice x64, local copies, waits for them, and re-layouts, forward_row(): pivot = lax.dynamic_slice_in_dim(factor_row, row, 1, 0)[0]  37.1 us
    dynamic_slice x64, local copies, waits for them, and re-layouts, backward_row(): pivot = lax.dynamic_slice_in_dim(factor_col, row, 1, 0)[0]  37.1 us
    psum x1, blocking collectives, local(): gram_matrix, cross_matrix = lax.psum((gram_part, cross_part), 'slab')  26.3 us
    ppermute x2, waiting for transfers between devices, gather_around(): earlier.append(lax.ppermute(earlier[-1], axis, up))  21.2 us
  transfers between devices with their start and end apart: 9, of which 4 were waited for; matrix products, arithmetic and copies ran while one was open for 55% of the time, Pallas kernels for 0%

profile of v1, /device:TPU:0, one launch (start us, length us, event | category | flops | bytes accessed | tf_op | source)
XLA Modules:
  0.0 432.1 jit_solution(11044820400536317919)
XLA Ops:
  6.5 1.6 fusion.81
  8.1 3.0 collective-permute-start
  11.1 1.3 collective-permute-start.1
  12.4 1.3 fusion.78
  13.7 1.4 fusion.79
  15.2 1.0 fusion.80
  16.2 0.7 fusion.77
  16.9 0.9 convert_multiply_fusion
  18.5 1.3 reshape.81
  21.2 1.4 div.111
  23.1 2.0 fusion.55
  25.8 4.6 %collective-permute-start.2 = (f32[16,1,8,128]{3,2,1,0:T(8,128)S(1)}, f32[16,1,8,128]{3,2,1,0:T(8,128)S(1)}, u32[]{:S(2)}, u32[]{:S(2)}) collective-permute-start(f32[16,1,8,128]{3,2,1,0:T(8,128)S(1)} %get-tuple-element.515), channel_id=1, source_target_pairs={{0,1},{1,2},{2,3},{3,4},{4,5},{5,6},{6,7},{8,9},{9,10},{10,11},{11... | collective-permute-start | bytes 196616 | tf_op jit(solution)/shard_map/ppermute | solution.py:31
  30.4 1.3 collective-permute-start.3
  31.8 3.0 collective-permute-done.3
  34.8 0.8 fusion.39
  35.7 31.1 %while.62 = (s32[]{:T(128)}, f32[12,16,512]{2,1,0:T(8,128)S(1)}, s32[12,512]{1,0:T(8,128)}, f32[16,64,128]{2,1,0:T(8,128)S(1)}, s32[]{:T(128)}) while((s32[]{:T(128)}, f32[12,16,512]{2,1,0:T(8,128)S(1)}, s32[12,512]{1,0:T(8,128)}, f32[16,64,128]{2,1,0:T(8,128)S(1)}, s32[]{:T(128)}) %tuple.166), condition=%wide.region_2.3_spmd.clone, body=%wide.region_0.2_spmd.clone.sunk | while | flops 806489600 | bytes 901193 | solution.py:150
  35.7 0.8 and_select_fusion.4
  36.5 0.7 and_select_fusion.5
  37.2 1.0 fusion.110
  38.3 0.7 and_select_fusion.4
  39.1 0.7 and_select_fusion.5
  39.8 1.0 fusion.110
  40.9 0.7 and_select_fusion.4
  41.7 0.7 and_select_fusion.5
  42.4 1.0 fusion.110
  43.5 0.7 and_select_fusion.4
  44.2 0.7 and_select_fusion.5
  45.0 1.1 fusion.110
  46.1 0.7 and_select_fusion.4
  46.8 0.7 and_select_fusion.5
  47.6 1.0 fusion.110
  48.7 0.7 and_select_fusion.4
  49.4 0.7 and_select_fusion.5
  50.2 1.0 fusion.110
  51.3 0.7 and_select_fusion.4
  52.0 0.7 and_select_fusion.5
  52.8 1.1 fusion.110
  54.6 0.7 and_select_fusion.5
  55.3 1.0 fusion.110
  56.4 0.7 and_select_fusion.4
  57.2 0.7 and_select_fusion.5
  57.9 1.0 fusion.110
  59.8 0.7 and_select_fusion.5
  60.5 1.1 fusion.110
  62.3 0.7 and_select_fusion.5
  63.1 1.0 fusion.110
  64.9 0.7 and_select_fusion.5
  65.7 1.0 fusion.110
  66.9 16.3 %psum.21 = f32[6144]{0:T(1024)S(1)} all-reduce(f32[6144]{0:T(1024)S(1)} %reduce_sum.24), channel_id=1, replica_groups=mesh['grp'=4,'slab'=8] {'grp'}, use_global_device_ids=true, to_apply=%region_4.5 | all-reduce | flops 6144 | bytes 49152 | tf_op jit(solution)/shard_map/psum | solution.py:180
  83.3 0.9 subtract_multiply_fusion
  84.3 11.2 %collective-permute-done.4 = f32[16,6144]{1,0:T(8,128)S(1)} collective-permute-done((f32[16,6144]{1,0:T(8,128)S(1)}, f32[16,6144]{1,0:T(8,128)S(1)}, u32[]{:S(2)}, u32[]{:S(2)}) %collective-permute-start.4) | collective-permute-done | bytes 393248 | tf_op jit(solution)/shard_map/ppermute | solution.py:17
  95.4 2.9 collective-permute-start.6
  98.4 1.1 copy.20
  99.5 10.0 %collective-permute-done.5 = f32[16,6144]{1,0:T(8,128)S(1)} collective-permute-done((f32[16,6144]{1,0:T(8,128)S(1)}, f32[16,6144]{1,0:T(8,128)S(1)}, u32[]{:S(2)}, u32[]{:S(2)}) %collective-permute-start.5) | collective-permute-done | bytes 393248 | tf_op jit(solution)/shard_map/ppermute | solution.py:17
  109.6 13.6 %collective-permute-done.6 = f32[16,6144]{1,0:T(8,128)S(1)} collective-permute-done((f32[16,6144]{1,0:T(8,128)S(1)}, f32[16,6144]{1,0:T(8,128)S(1)}, u32[]{:S(2)}, u32[]{:S(2)}) %collective-permute-start.6) | collective-permute-done | bytes 393248 | tf_op jit(solution)/shard_map/ppermute | solution.py:19
  123.4 1.6 copy-done.1
  125.1 1.4 fusion.26
  126.5 3.3 fusion.28
  129.8 26.3 %all-reduce = (f32[64,64]{1,0:T(8,128)S(1)}, f32[64,64]{1,0:T(8,128)S(1)}) all-reduce(f32[64,64]{1,0:T(8,128)S(1)} %fusion.28, f32[64,64]{1,0:T(8,128)S(1)} %fusion.26), channel_id=1, replica_groups=mesh['grp'=4,'slab'=8] {'slab'}, use_global_device_ids=true, to_apply=%region_8.9 | all-reduce | flops 8192 | bytes 65536 | tf_op jit(solution)/shard_map/psum | solution.py:187
  156.2 94.8 %while.63 = (s32[]{:T(128)}, f32[64,64]{1,0:T(8,128)S(1)}, f32[64,64]{0,1:T(8,128)S(1)}, s32[]{:T(128)}, s32[]{:T(128)}) while((s32[]{:T(128)}, f32[64,64]{1,0:T(8,128)S(1)}, f32[64,64]{0,1:T(8,128)S(1)}, s32[]{:T(128)}, s32[]{:T(128)}) %tuple.153), condition=%wide.region_7.8_spmd.clone.clone, body=%wide.region_6.7_spmd.clone.clone.sunk | while | flops 65923 | bytes 101992 | solution.py:76
  251.1 84.9 %while.60 = (s32[]{:T(128)}, f32[64,64]{1,0:T(8,128)S(1)}, f32[64,64]{1,0:T(8,128)S(1)}, f32[64,64]{1,0:T(8,128)S(1)}, s32[]{:T(128)}, /*index=5*/s32[]{:T(128)}, s32[]{:T(128)}) while((s32[]{:T(128)}, f32[64,64]{1,0:T(8,128)S(1)}, f32[64,64]{1,0:T(8,128)S(1)}, f32[64,64]{1,0:T(8,128)S(1)}, s32[]{:T(128)}, /*index=5*/s32[]{:T(128)}, ...), condition=%wide.region_10.11_spmd, body=%wide.region_9.10_spmd.sunk | while | flops 49283 | bytes 36205 | solution.py:93
  336.0 85.4 %while.61 = (s32[]{:T(128)}, f32[64,64]{1,0:T(8,128)S(1)}, f32[64,64]{1,0:T(8,128)S(1)}, f32[64,64]{0,1:T(8,128)S(1)}, s32[]{:T(128)}, /*index=5*/s32[]{:T(128)}, s32[]{:T(128)}, s32[]{:T(128)}) while((s32[]{:T(128)}, f32[64,64]{1,0:T(8,128)S(1)}, f32[64,64]{1,0:T(8,128)S(1)}, f32[64,64]{0,1:T(8,128)S(1)}, s32[]{:T(128)}, ...), condition=%wide.region_12.13_spmd, body=%wide.region_11.12_spmd.sunk | while | flops 49287 | bytes 35751 | solution.py:111
  421.5 2.9 fusion.30
  424.4 0.9 copy.16
  (863 shorter events, 228.3 us)
Async XLA Ops:
  6.5 8.6 %copy-start = (f32[16,8,8,128]{3,2,1,0:T(8,128)S(1)}, f32[16,8,8,128]{3,2,1,0:T(8,128)}, u32[]{:S(2)}) copy-start(f32[16,8,8,128]{3,2,1,0:T(8,128)} %param.16) | copy-start | bytes 1572868
  6.5 119.9 %all-gather.3.cloned.1.call-start = ((), (), s32[]{:S(2)}) async-start(), calls=%async_computation | async-start | bytes 1966080 | tf_op jit(solution)/shard_map/all_gather | solution.py:184
  8.1 15.0 %collective-permute-start = (f32[16,1,8,128]{3,2,1,0:T(8,128)}, f32[16,1,8,128]{3,2,1,0:T(8,128)}, u32[]{:S(2)}, u32[]{:S(2)}) collective-permute-start(f32[16,1,8,128]{3,2,1,0:T(8,128)} %get-tuple-element.525), channel_id=1, source_target_pairs={{0,1},{1,2},{2,3},{3,4},{4,5},{5,6},{6,7},{8,9},{9,10},{10,11},{11... | collective-permute-start | bytes 196616 | tf_op jit(solution)/shard_map/ppermute | solution.py:31
  11.1 12.0 %collective-permute-start.1 = (f32[16,1,8,128]{3,2,1,0:T(8,128)}, f32[16,1,8,128]{3,2,1,0:T(8,128)}, u32[]{:S(2)}, u32[]{:S(2)}) collective-permute-start(f32[16,1,8,128]{3,2,1,0:T(8,128)} %get-tuple-element.526), channel_id=1, source_target_pairs={{1,0},{2,1},{3,2},{4,3},{5,4},{6,5},{7,6},{9,8},{10,9},{11,10},{12... | collective-permute-start | bytes 196616 | tf_op jit(solution)/shard_map/ppermute | solution.py:32
  25.1 9.6 %copy-start.3 = (f32[8,8,128]{2,1,0:T(8,128)S(1)}, f32[8,8,128]{2,1,0:T(8,128)}, u32[]{:S(2)}) copy-start(f32[8,8,128]{2,1,0:T(8,128)} %get-tuple-element.529) | copy-start | bytes 98308
  25.1 9.6 %copy-start.4 = (f32[8,8,128]{2,1,0:T(8,128)S(1)}, f32[8,8,128]{2,1,0:T(8,128)}, u32[]{:S(2)}) copy-start(f32[8,8,128]{2,1,0:T(8,128)} %get-tuple-element.530) | copy-start | bytes 98308
  25.2 9.6 %copy-start.5 = (f32[8,8,128]{2,1,0:T(8,128)S(1)}, f32[8,8,128]{2,1,0:T(8,128)}, u32[]{:S(2)}) copy-start(f32[8,8,128]{2,1,0:T(8,128)} %get-tuple-element.531) | copy-start | bytes 98308
  25.2 9.6 %copy-start.6 = (f32[8,8,128]{2,1,0:T(8,128)S(1)}, f32[8,8,128]{2,1,0:T(8,128)}, u32[]{:S(2)}) copy-start(f32[8,8,128]{2,1,0:T(8,128)} %get-tuple-element.532) | copy-start | bytes 98308
  25.2 9.6 %copy-start.7 = (f32[8,8,128]{2,1,0:T(8,128)S(1)}, f32[8,8,128]{2,1,0:T(8,128)}, u32[]{:S(2)}) copy-start(f32[8,8,128]{2,1,0:T(8,128)} %get-tuple-element.533) | copy-start | bytes 98308
  25.2 9.6 %copy-start.8 = (f32[8,8,128]{2,1,0:T(8,128)S(1)}, f32[8,8,128]{2,1,0:T(8,128)}, u32[]{:S(2)}) copy-start(f32[8,8,128]{2,1,0:T(8,128)} %get-tuple-element.534) | copy-start | bytes 98308
  25.2 9.6 %copy-start.9 = (f32[8,8,128]{2,1,0:T(8,128)S(1)}, f32[8,8,128]{2,1,0:T(8,128)}, u32[]{:S(2)}) copy-start(f32[8,8,128]{2,1,0:T(8,128)} %param.18) | copy-start | bytes 98308
  25.8 6.0 %collective-permute-start.2 = (f32[16,1,8,128]{3,2,1,0:T(8,128)S(1)}, f32[16,1,8,128]{3,2,1,0:T(8,128)S(1)}, u32[]{:S(2)}, u32[]{:S(2)}) collective-permute-start(f32[16,1,8,128]{3,2,1,0:T(8,128)S(1)} %get-tuple-element.515), channel_id=1, source_target_pairs={{0,1},{1,2},{2,3},{3,4},{4,5},{5,6},{6,7},{8,9},{9,10},{10,11},{11... | collective-permute-start | bytes 196616 | tf_op jit(solution)/shard_map/ppermute | solution.py:31
  30.4 4.4 %collective-permute-start.3 = (f32[16,1,8,128]{3,2,1,0:T(8,128)S(1)}, f32[16,1,8,128]{3,2,1,0:T(8,128)S(1)}, u32[]{:S(2)}, u32[]{:S(2)}) collective-permute-start(f32[16,1,8,128]{3,2,1,0:T(8,128)S(1)} %get-tuple-element.516), channel_id=1, source_target_pairs={{1,0},{2,1},{3,2},{4,3},{5,4},{6,5},{7,6},{9,8},{10,9},{11,10},{12... | collective-permute-start | bytes 196616 | tf_op jit(solution)/shard_map/ppermute | solution.py:32
  35.6 31.2 %copy-start.10 = (f32[12,512]{1,0:T(8,128)S(1)}, f32[12,512]{1,0:T(8,128)}, u32[]{:S(2)}) copy-start(f32[12,512]{1,0:T(8,128)} %fusion.65) | copy-start | bytes 73732
  35.6 31.2 %copy-start.11 = (f32[12,512]{1,0:T(8,128)S(1)}, f32[12,512]{1,0:T(8,128)}, u32[]{:S(2)}) copy-start(f32[12,512]{1,0:T(8,128)} %div.111) | copy-start | bytes 73732
  35.7 47.6 %copy-start.2 = (f32[16,6144]{1,0:T(8,128)S(1)}, f32[16,6144]{1,0:T(8,128)}, u32[]{:S(2)}) copy-start(f32[16,6144]{1,0:T(8,128)} %param.23) | copy-start | bytes 1179652
  35.7 47.6 %copy-start.12 = (f32[6144]{0:T(1024)S(1)}, f32[6144]{0:T(1024)}, u32[]{:S(2)}) copy-start(f32[6144]{0:T(1024)} %param.22) | copy-start | bytes 73732
  35.7 47.6 %copy-start.13 = (f32[6144]{0:T(1024)S(1)}, f32[6144]{0:T(1024)}, u32[]{:S(2)}) copy-start(f32[6144]{0:T(1024)} %fusion.66) | copy-start | bytes 73732
  35.7 47.6 %copy-start.14 = (f32[6144]{0:T(1024)S(1)}, f32[6144]{0:T(1024)}, u32[]{:S(2)}) copy-start(f32[6144]{0:T(1024)} %param.21) | copy-start | bytes 73732
  84.2 337.3 %all-gather.5.cloned.1.call-start = ((), (), s32[]{:S(2)}) async-start(), calls=%async_computation.1 | async-start | bytes 2621440 | tf_op jit(solution)/shard_map/all_gather | solution.py:193
  84.2 11.2 %collective-permute-start.4 = (f32[16,6144]{1,0:T(8,128)S(1)}, f32[16,6144]{1,0:T(8,128)S(1)}, u32[]{:S(2)}, u32[]{:S(2)}) collective-permute-start(f32[16,6144]{1,0:T(8,128)S(1)} %get-tuple-element.527), channel_id=1, source_target_pairs={{0,8},{8,16},{16,24},{24,0},{1,9},{9,17},{17,25},{25,1},{2,10},{10... | collective-permute-start | bytes 1179656 | tf_op jit(solution)/shard_map/ppermute | solution.py:17
  95.4 14.1 %collective-permute-start.5 = (f32[16,6144]{1,0:T(8,128)S(1)}, f32[16,6144]{1,0:T(8,128)S(1)}, u32[]{:S(2)}, u32[]{:S(2)}) collective-permute-start(f32[16,6144]{1,0:T(8,128)S(1)} %collective-permute-done.4), channel_id=1, source_target_pairs={{0,8},{8,16},{16,24},{24,0},{1,9},{9,17},{17,25},{25,1},{2,10},{10... | collective-permute-start | bytes 1179656 | tf_op jit(solution)/shard_map/ppermute | solution.py:17
  95.4 27.8 %collective-permute-start.6 = (f32[16,6144]{1,0:T(8,128)S(1)}, f32[16,6144]{1,0:T(8,128)S(1)}, u32[]{:S(2)}, u32[]{:S(2)}) collective-permute-start(f32[16,6144]{1,0:T(8,128)S(1)} %get-tuple-element.527), channel_id=1, source_target_pairs={{0,24},{8,0},{16,8},{24,16},{1,25},{9,1},{17,9},{25,17},{2,26},{10... | collective-permute-start | bytes 1179656 | tf_op jit(solution)/shard_map/ppermute | solution.py:19
  123.4 1.6 copy-start.1
Sparse Core Ops, SparseCore 0:
  84.3 40.5 all-gather.2
  126.7 34.2 all-gather.4
